TPU v7x, 256 devices: a whole 4x4x8 slice. The times are simulated.
256 devices in a mesh: ab: 128 (over z, y, x_hi, core), ij: 2 (over x_lo).
Axes of the slice: x: 4 (x_hi: 2, x_lo: 2; x = x_hi * 2 + x_lo), y: 4, z: 8, core: 2. Of those that a mesh axis runs over, the one named last changes fastest.
Arguments:
- amplitudes: float32 [1024, 2048], P('ab', 'ij'), may hold values from -6 to 6
- integrals: float32 [131072, 2048], P('ab'), may hold values from -0.125 to 0.125
- occ_pairs: float32 [1024], P(('ab', 'ij')), may hold values from -2 to -0.5
- vir_pairs: float32 [131072], P('ab'), may hold values from 1 to 4
Outputs:
- update: float32 [1024, 131072], P(('ab', 'ij'))
All inputs are finite; a program needn't handle non-finite values.
Results may differ from a plain program's by a relative error of at most 0.00007.
Values sent between devices are 32-bit elements; how exact they have to be, the bound alone decides.
A program may use at most 64 MiB of HBM per device.

v0:
```python
import jax
import jax.numpy as jnp
from jax import lax
from jax.sharding import Mesh
from jax.sharding import PartitionSpec as P

AB = ("ab_0", "ab_1", "ab_2", "ab_3")
AB_IJ = ("ab_0", "ab_1", "ab_2", "ab_3", "ij")


def copy_for_each(array, axis):
    count = lax.axis_size(axis)
    return lax.all_to_all(
        jnp.broadcast_to(array[None], (count, *array.shape)), axis, 0, 0, tiled=True
    )


def in_order(tiles, dim):
    dims = list(tiles.shape[1:])
    dims[dim] *= tiles.shape[0]
    return jnp.moveaxis(tiles, 0, dim).reshape(dims)


def gathered_by_axis(array, axes, dim):
    far, near = axes
    first = copy_for_each(array, far)
    tiles = jnp.swapaxes(copy_for_each(first, near), 0, 1)
    return in_order(tiles.reshape(-1, *array.shape), dim)


def contract(block_amps, integrals):
    return lax.dot_general(
        block_amps,
        integrals,
        (((1,), (1,)), ((), ())),
        precision=lax.Precision.HIGHEST,
        preferred_element_type=jnp.float32,
    )


def shards(amplitudes, integrals, occ_pairs, vir_pairs):
    arrived = lax.all_to_all(amplitudes, "ij", split_axis=0, concat_axis=1, tiled=True)
    slice_amps = gathered_by_axis(arrived, (("ab_0", "ab_1", "ab_2"), "ab_3"), 0)
    row_energy = gathered_by_axis(occ_pairs, (("ab_0", "ab_1", "ab_2"), "ab_3"), 0)
    groups = lax.axis_size(AB)
    per_device = occ_pairs.shape[0]
    panel_cols = integrals.shape[1]
    grouped = slice_amps.reshape(groups, per_device, panel_cols)
    energy_grouped = row_energy.reshape(groups, per_device)
    block_amps = grouped.reshape(-1, panel_cols)
    residual = contract(block_amps, integrals)
    block_energy = energy_grouped.reshape(-1)
    residual = residual / (vir_pairs[None, :] - block_energy[:, None])
    moved = lax.all_to_all(residual, AB, split_axis=0, concat_axis=1, tiled=True)
    return moved


def solution(mesh):
    finer = Mesh(
        mesh.devices.reshape(8, 4, 2, 2, mesh.shape["ij"]), ("ab_0", "ab_1", "ab_2", "ab_3", "ij")
    )
    in_specs = (P(AB, "ij"), P(AB, None), P(AB_IJ), P(AB))
    out_specs = P(AB_IJ, None)
    return jax.shard_map(
        shards, mesh=finer, in_specs=in_specs, out_specs=out_specs, check_vma=False
    )
```

profile of v0, /device:TPU:1, one launch (start us, length us, event | category | flops | bytes accessed | tf_op | source)
XLA Modules:
  0.0 192.7 jit_solution(120994332012294861)
XLA Ops:
  0.0 1.3 broadcast_in_dim.15
  1.3 15.1 %all-to-all-start.3 = ((f32[64,1,4]{2,1,0:T(1,128)}), f32[64,1,4]{2,1,0:T(1,128)S(1)}, u32[]{:S(2)}, u32[]{:S(2)}) async-start(f32[64,1,4]{2,1,0:T(1,128)} %broadcast_in_dim.15), calls=%async_computation.3 | async-start | bytes 65536 | tf_op jit(solution)/shard_map/all_to_all | solution.py:13
  16.4 0.8 all_to_all.39
  17.2 10.0 %all-to-all-done.3 = f32[64,1,4]{2,1,0:T(1,128)S(1)} async-done(((f32[64,1,4]{2,1,0:T(1,128)}), f32[64,1,4]{2,1,0:T(1,128)S(1)}, u32[]{:S(2)}, u32[]{:S(2)}) %all-to-all-start.3) | async-done | bytes 1056 | tf_op jit(solution)/shard_map/all_to_all | solution.py:13
  27.1 0.1 copy.8
  27.2 0.1 reshape.19
  27.3 5.5 %all_to_all.56 = f32[2,1,256]{2,1,0:T(1,128)S(1)} all-to-all(f32[2,1,256]{2,1,0:T(1,128)S(1)} %reshape.19), channel_id=1, replica_groups=mesh['ab_0'=8,'ab_1'=4,'ab_2'=2,'ab_3'=2,'ij'=2] {'ab_3'}, dimensions={0} | all-to-all | bytes 4096 | tf_op jit(solution)/shard_map/all_to_all | solution.py:13
  32.8 5.1 %all_to_all.57 = f32[2,4,1024]{2,1,0:T(4,128)S(1)} all-to-all(f32[2,4,1024]{2,1,0:T(4,128)S(1)} %all_to_all.39), channel_id=1, replica_groups=mesh['ab_0'=8,'ab_1'=4,'ab_2'=2,'ab_3'=2,'ij'=2] {'ij'}, dimensions={0} | all-to-all | bytes 65536 | tf_op jit(solution)/shard_map/all_to_all | solution.py:42
  37.9 1.8 broadcast_in_dim.13
  39.7 4.7 %all-to-all-start.1 = ((f32[64,4,2048]{2,1,0:T(4,128)}), f32[64,4,2048]{2,1,0:T(4,128)S(1)}, u32[]{:S(2)}, u32[]{:S(2)}) async-start(f32[64,4,2048]{2,1,0:T(4,128)} %broadcast_in_dim.13), calls=%async_computation.1 | async-start | bytes 4194304 | tf_op jit(solution)/shard_map/all_to_all | solution.py:13
  44.4 0.6 broadcast.5
  45.0 0.6 reduce
  45.7 0.1 reshape.20
  45.8 0.1 copy.9
  45.9 0.1 sub.16
  46.0 47.0 %all-to-all-done.1 = f32[64,4,2048]{2,1,0:T(4,128)S(1)} async-done(((f32[64,4,2048]{2,1,0:T(4,128)}), f32[64,4,2048]{2,1,0:T(4,128)S(1)}, u32[]{:S(2)}, u32[]{:S(2)}) %all-to-all-start.1) | async-done | bytes 2097184 | tf_op jit(solution)/shard_map/all_to_all | solution.py:13
  93.1 1.0 broadcast_in_dim.14
  94.1 11.7 %all_to_all.58 = f32[2,64,4,2048]{3,2,1,0:T(4,128)S(1)} all-to-all(f32[2,64,4,2048]{3,2,1,0:T(4,128)S(1)} %broadcast_in_dim.14), channel_id=1, replica_groups=mesh['ab_0'=8,'ab_1'=4,'ab_2'=2,'ab_3'=2,'ij'=2] {'ab_3'}, dimensions={0} | all-to-all | bytes 8388608 | tf_op jit(solution)/shard_map/all_to_all | solution.py:13
  105.8 2.2 %copy.7 = f32[64,2,4,2048]{3,2,1,0:T(4,128)} copy(f32[64,2,4,2048]{3,2,0,1:T(4,128)S(1)} %bitcast.16) | data formatting | bytes 8388608 | tf_op jit(solution)/shard_map/transpose | solution.py:27
  108.0 0.0 copy-start
  108.0 5.3 %reshape_reshape_reshape_reshape.3 = f32[512,2048]{1,0:T(8,128)} reshape(f32[64,2,4,2048]{3,2,1,0:T(4,128)} %copy.7) | data formatting | bytes 8388608 | tf_op jit(solution)/shard_map/reshape;reshape;reshape;reshape | solution.py:50
  113.3 0.0 copy-done
  113.3 17.9 %subtract_divide_fusion = f32[512,1024]{1,0:T(8,128)} fusion(f32[512,2048]{1,0:T(8,128)} %reshape_reshape_reshape_reshape.3, f32[1024,2048]{1,0:T(8,128)} %param.5, f32[512]{0:T(512)S(1)} %sub.16, f32[1024]{0:T(1024)S(1)} %copy-done), kind=kOutput, calls=%fused_computation | convolution fusion | flops 12885950464 | bytes 14686208 | tf_op jit(solution)/shard_map/dot_general | solution.py:32
  131.2 1.9 all_to_all.46
  133.1 58.3 %all_to_all.59 = f32[128,4,1024]{2,1,0:T(4,128)S(1)} all-to-all(f32[128,4,1024]{2,1,0:T(4,128)S(1)} %all_to_all.46), channel_id=1, replica_groups=mesh['ab_0'=8,'ab_1'=4,'ab_2'=2,'ab_3'=2,'ij'=2] {'ab_0','ab_1','ab_2','..., dimensions={0} | all-to-all | bytes 4194304 | tf_op jit(solution)/shard_map/all_to_all | solution.py:54
  191.4 1.3 copy.12
  (2 shorter events, 0.0 us)
Async XLA Ops:
  1.3 25.9 %all-to-all-start.3 = ((f32[64,1,4]{2,1,0:T(1,128)}), f32[64,1,4]{2,1,0:T(1,128)S(1)}, u32[]{:S(2)}, u32[]{:S(2)}) async-start(f32[64,1,4]{2,1,0:T(1,128)} %broadcast_in_dim.15), calls=%async_computation.3 | async-start | bytes 65536 | tf_op jit(solution)/shard_map/all_to_all | solution.py:13
  39.7 53.3 %all-to-all-start.1 = ((f32[64,4,2048]{2,1,0:T(4,128)}), f32[64,4,2048]{2,1,0:T(4,128)S(1)}, u32[]{:S(2)}, u32[]{:S(2)}) async-start(f32[64,4,2048]{2,1,0:T(4,128)} %broadcast_in_dim.13), calls=%async_computation.1 | async-start | bytes 4194304 | tf_op jit(solution)/shard_map/all_to_all | solution.py:13
  108.0 5.3 %copy-start = (f32[1024]{0:T(1024)S(1)}, f32[1024]{0:T(1024)}, u32[]{:S(2)}) copy-start(f32[1024]{0:T(1024)} %param.7) | copy-start | bytes 12292
where the time goes:
time: 194 us; the launch traced here: 193 us
  blocking collectives  80.6 us (42%)
  waiting for transfers between devices  57 us (29%)
  starting transfers between devices  19.8 us (10%)
  matrix products  17.9 us (9%)
  local copies, waits for them, and re-layouts  16.7 us (9%)
    all_to_all x1, blocking collectives, shards(): lax.all_to_all(residual, AB, split_axis=0, concat_axis=1, tiled=True)  58.3 us
    all_to_all x2, waiting for transfers between devices, copy_for_each(): lax.all_to_all(jnp.broadcast_to(array[None], (count, *array.shape)), axis...  57 us
    all_to_all x2, starting transfers between devices, copy_for_each(): lax.all_to_all(jnp.broadcast_to(array[None], (count, *array.shape)), axis...  19.8 us
    dot_general x1, matrix products, contract(): lax.dot_general(block_amps, integrals, (((1,), (1,)), ((), ())), precisio...  17.9 us
    all_to_all x2, blocking collectives, copy_for_each(): lax.all_to_all(jnp.broadcast_to(array[None], (count, *array.shape)), axis...  17.1 us
    another operation x1, local copies, waits for them, and re-layouts, shards(): block_amps = grouped.reshape(-1, panel_cols)  5.3 us
    all_to_all x1, blocking collectives, shards(): lax.all_to_all(amplitudes, 'ij', split_axis=0, concat_axis=1, tiled=True)  5.14 us
    broadcast_in_dim x4, local copies, waits for them, and re-layouts, copy_for_each(): jnp.broadcast_to(array[None], (count, *array.shape))  4.22 us
  transfers between devices with their start and end apart: 2, of which 2 were waited for; matrix products, arithmetic and copies ran while one was open for 1% of the time, Pallas kernels for 0%

commit v1 on v0

v1 whole, which is shorter than its diff:
```python
import functools

import jax
import jax.numpy as jnp
from jax import lax
from jax.experimental import pallas as pl
from jax.experimental.pallas import tpu as pltpu
from jax.sharding import Mesh
from jax.sharding import PartitionSpec as P

AXES = ("z", "y", "xh", "c", "xl")
MESH = pl.DeviceIdType.MESH
NT = (((1,), (1,)), ((), ()))

DIST = (4, 3, 5, 2, 6, 1, 7, 0)
GROUPS = ((0, 1), (1, 2), (3, 2), (5, 2), (7, 1))
NG = len(GROUPS)
PIECES = 8


def split(x):
    hi = x.astype(jnp.bfloat16)
    lo = (x - hi.astype(jnp.float32)).astype(jnp.bfloat16)
    return hi, lo


def kernel(
    amp_ref, int_ref, occ_ref, vir_ref, out_ref,
    flat, etile, gath, ener, stage, bhi, blo, acat, res,
    b_sem, z_send, z_recv, y_send, y_recv, x_send, x_recv, c_send, c_recv,
    e_send, e_recv, r_send, r_recv, own_sem,
):
    z, y, xh, c, xl = (lax.axis_index(a) for a in AXES)
    block = ((z * 4 + y) * 2 + xh) * 2 + c
    q_me = c * 8 + xh * 4 + y
    partner = (z, y, 1 - xh, c, 1 - xl)
    sibling = (z, y, xh, 1 - c, xl)

    def piece(i):
        rows = pl.ds(i * 128, 128)
        return pltpu.make_async_copy(int_ref.at[rows, :], stage.at[rows, :], b_sem.at[i])

    for i in range(PIECES):
        piece(i).start()

    barrier = pltpu.get_barrier_semaphore()
    peers = [(lax.rem(z + d, 8), y, xh, c, xl) for d in range(1, 8)]
    peers += [(lax.rem(z + d, 8), y, xh, c, 1 - xl) for d in range(8)]
    peers += [(z, lax.rem(y + d, 4), xh, c, xl) for d in range(1, 4)]
    peers += [partner, sibling]
    for peer in peers:
        pl.semaphore_signal(barrier, inc=1, device_id=peer, device_id_type=MESH)

    for s in range(8):
        flat[pl.ds(s, 8, stride=8), :] = amp_ref[:, pl.ds(s * 128, 128)]
    lane_row = lax.broadcasted_iota(jnp.int32, (8, 128), 0)
    energy = jnp.where(lane_row % 4 == 0, occ_ref[0], occ_ref[1])
    energy = jnp.where(lane_row % 4 == 2, occ_ref[2], energy)
    energy = jnp.where(lane_row % 4 == 3, occ_ref[3], energy)
    etile[...] = energy
    ener[7, pl.ds(pl.multiple_of(q_me * 8, 8), 8), :] = energy
    gath[7, xl, pl.ds(pl.multiple_of(q_me * 32, 32), 32), :] = flat[
        pl.ds(pl.multiple_of(xl * 32, 32), 32), :
    ]

    def prepare(i):
        piece(i).wait()

        def body(j, carry):
            rows = pl.ds(pl.multiple_of(i * 128 + j * 16, 16), 16)
            hi, lo = split(stage[rows, :])
            bhi[rows, :] = hi
            blo[rows, :] = lo
            return carry

        lax.fori_loop(0, 8, body, 0)

    prepare(0)
    pl.semaphore_wait(barrier, len(peers))

    def remote(src, dst, send, recv, device):
        return pltpu.make_async_remote_copy(
            src_ref=src, dst_ref=dst, send_sem=send, recv_sem=recv,
            device_id=device, device_id_type=MESH,
        )

    e_rows = pl.ds(pl.multiple_of(q_me * 8, 8), 8)
    a_rows = pl.ds(pl.multiple_of(q_me * 32, 32), 32)
    group_of = [g for g, (first, n) in enumerate(GROUPS) for _ in range(n)]
    for k, d in enumerate(DIST):
        zd = lax.rem(z + 8 - d, 8)
        if d:
            remote(
                etile, ener.at[k, e_rows, :], e_send.at[0], e_recv.at[0], (zd, y, xh, c, xl)
            ).start()
    for k, d in enumerate(DIST):
        zd = lax.rem(z + 8 - d, 8)
        for j in ((xl, 1 - xl) if d else (1 - xl,)):
            remote(
                flat.at[pl.ds(pl.multiple_of(j * 32, 32), 32), :],
                gath.at[k, xl, a_rows, :],
                z_send, z_recv.at[group_of[k]], (zd, y, xh, c, j),
            ).start()

    x_rows = pl.ds(pl.multiple_of((c * 8 + xh * 4) * 32, 128), 128)
    c_rows = pl.ds(pl.multiple_of(c * 256, 256), 256)
    ex_rows = pl.ds(pl.multiple_of((c * 8 + xh * 4) * 8, 32), 32)
    ec_rows = pl.ds(pl.multiple_of(c * 64, 64), 64)

    def slots(g):
        first, n = GROUPS[g]
        return pl.ds(first, n)

    def take(ref, recv):
        remote(ref, ref, own_sem, recv, sibling).wait_recv()

    def z_to_y(g):
        if g == NG - 1:
            take(gath.at[slots(g), 0, pl.ds(0, 32), :], z_recv.at[g])
        else:
            take(gath.at[slots(g), :, pl.ds(0, 32), :], z_recv.at[g])
        if g == 0:
            take(ener.at[0, pl.ds(0, 56), :], e_recv.at[0])
        for d in (2, 1, 3):
            peer = (z, lax.rem(y + d, 4), xh, c, xl)
            mine = gath.at[slots(g), :, a_rows, :]
            remote(mine, mine, y_send, y_recv.at[g], peer).start()
            if g == 0:
                mine = ener.at[:, e_rows, :]
                remote(mine, mine, e_send.at[1], e_recv.at[1], peer).start()

    def y_to_x(g):
        take(gath.at[slots(g), :, pl.ds(0, 96), :], y_recv.at[g])
        mine = gath.at[slots(g), :, x_rows, :]
        remote(mine, mine, x_send, x_recv.at[g], partner).start()
        if g == 0:
            take(ener.at[:, pl.ds(0, 24), :], e_recv.at[1])
            mine = ener.at[:, ex_rows, :]
            remote(mine, mine, e_send.at[2], e_recv.at[2], partner).start()

    def x_to_c(g):
        take(gath.at[slots(g), :, pl.ds(0, 128), :], x_recv.at[g])
        mine = gath.at[slots(g), :, c_rows, :]
        remote(mine, mine, c_send, c_recv.at[g], sibling).start()
        if g == 0:
            take(ener.at[:, pl.ds(0, 32), :], e_recv.at[2])
            mine = ener.at[:, ec_rows, :]
            remote(mine, mine, e_send.at[3], e_recv.at[3], sibling).start()

    upper = lax.broadcasted_iota(jnp.int32, (8, 8, 128), 1) < 4
    home = pl.ds(pl.multiple_of(block * 32, 32), 32)

    def multiply(g):
        first, n = GROUPS[g]
        m = 64 * n
        take(gath.at[slots(g), :, pl.ds(0, 256), :], c_recv.at[g])
        if g == 0:
            take(ener.at[:, pl.ds(0, 64), :], e_recv.at[3])
        for i in range(n):
            for h in range(2):
                for s in range(8):
                    hi, lo = split(gath[first + i, h, pl.ds(s, 64, stride=8), :])
                    cols = pl.ds((h * 8 + s) * 128, 128)
                    acat[pl.ds(64 * i, 64), cols] = hi
                    acat[pl.ds(m + 64 * i, 64), cols] = lo
        occ = []
        for i in range(n):
            pairs = ener[first + i].reshape(8, 2, 8, 128)
            occ.append(jnp.where(upper, pairs[:, 0], pairs[:, 1]))

        for nb in range(4):
            cols = pl.ds(nb * 256, 256)
            high = lax.dot_general(
                acat[pl.ds(0, 2 * m), :], bhi[cols, :], NT, preferred_element_type=jnp.float32
            )
            low = lax.dot_general(
                acat[pl.ds(0, m), :], blo[cols, :], NT, preferred_element_type=jnp.float32
            )
            total = high[:m] + (high[m:] + low)
            for i in range(n):
                tiles = []
                for t in range(2):
                    value = total[64 * i : 64 * i + 64, 128 * t : 128 * t + 128].reshape(8, 8, 128)
                    vir = vir_ref[pl.ds(nb * 2 + t, 1), :]
                    tiles.append(value / (vir[None] - occ[i]))
                even = jnp.where(upper, tiles[0], pltpu.roll(tiles[1], 4, 1))
                odd = jnp.where(upper, pltpu.roll(tiles[0], 4, 1), tiles[1])
                for b in range(8):
                    res[first + i, 2 * b, pl.ds(nb * 8, 8), :] = even[b]
                    res[first + i, 2 * b + 1, pl.ds(nb * 8, 8), :] = odd[b]

        for i in range(n):
            k = first + i
            zd = lax.rem(z + DIST[k], 8)

            def send(step, carry):
                q = lax.rem(q_me + step, 16)
                cd = q // 8
                xd = lax.rem(q // 4, 2)
                target = (zd, lax.rem(q, 4), xd, cd, lax.rem(xl + xd + 2 - xh, 2))
                remote(res.at[k, q], out_ref.at[home, :], r_send, r_recv, target).start()
                return carry

            lax.fori_loop(0 if DIST[k] else 1, 16, send, 0)

    z_to_y(0)
    prepare(1)
    prepare(2)
    z_to_y(1)
    y_to_x(0)
    prepare(3)
    prepare(4)
    prepare(5)
    z_to_y(2)
    y_to_x(1)
    x_to_c(0)
    prepare(6)
    prepare(7)
    z_to_y(3)
    z_to_y(4)
    multiply(0)
    y_to_x(2)
    x_to_c(1)
    y_to_x(3)
    multiply(1)
    x_to_c(2)
    y_to_x(4)
    x_to_c(3)
    multiply(2)
    x_to_c(4)
    multiply(3)
    multiply(4)

    own = pltpu.make_async_copy(res.at[7, q_me], out_ref.at[home, :], own_sem)
    own.start()
    own.wait()

    def sent(ref, send):
        remote(ref, ref, send, own_sem, sibling).wait_send()

    sent(gath.at[pl.ds(0, 7), :, pl.ds(0, 32), :], z_send)
    sent(flat.at[pl.ds(0, 32), :], z_send)
    sent(gath.at[:, :, pl.ds(0, 96), :], y_send)
    sent(gath.at[:, :, pl.ds(0, 128), :], x_send)
    sent(gath.at[:, :, pl.ds(0, 256), :], c_send)
    sent(ener.at[0, pl.ds(0, 56), :], e_send.at[0])
    sent(ener.at[:, pl.ds(0, 24), :], e_send.at[1])
    sent(ener.at[:, pl.ds(0, 32), :], e_send.at[2])
    sent(ener.at[:, pl.ds(0, 64), :], e_send.at[3])
    sent(out_ref.at[pl.ds(0, 127 * 32), :], r_send)
    take(out_ref.at[pl.ds(0, 127 * 32), :], r_recv)


def shards(amplitudes, integrals, occ_pairs, vir_pairs):
    f32, bf16 = jnp.float32, jnp.bfloat16
    dma = pltpu.SemaphoreType.DMA
    out = pl.pallas_call(
        kernel,
        out_shape=jax.ShapeDtypeStruct((4096, 128), f32),
        in_specs=[
            pl.BlockSpec(memory_space=pltpu.VMEM),
            pl.BlockSpec(memory_space=pl.ANY),
            pl.BlockSpec(memory_space=pltpu.SMEM),
            pl.BlockSpec(memory_space=pltpu.VMEM),
        ],
        out_specs=pl.BlockSpec(memory_space=pl.ANY),
        scratch_shapes=[
            pltpu.VMEM((64, 128), f32),
            pltpu.VMEM((8, 128), f32),
            pltpu.VMEM((8, 2, 512, 128), f32),
            pltpu.VMEM((8, 128, 128), f32),
            pltpu.VMEM((1024, 2048), f32),
            pltpu.VMEM((1024, 2048), bf16),
            pltpu.VMEM((1024, 2048), bf16),
            pltpu.VMEM((256, 2048), bf16),
            pltpu.VMEM((8, 16, 32, 128), f32),
            dma((PIECES,)),
            dma, dma((NG,)), dma, dma((NG,)), dma, dma((NG,)), dma, dma((NG,)),
            dma((4,)), dma((4,)), dma, dma, dma,
        ],
        compiler_params=pltpu.CompilerParams(
            collective_id=0, has_side_effects=True, vmem_limit_bytes=48 << 20
        ),
    )(amplitudes, integrals, occ_pairs, vir_pairs.reshape(8, 128))
    return out.reshape(1024, 4, 128).transpose(1, 0, 2).reshape(4, 131072)


def solution(mesh):
    finer = Mesh(mesh.devices.reshape(8, 4, 2, 2, 2), AXES)
    ab = ("z", "y", "xh", "c")
    in_specs = (P(ab, "xl"), P(ab, None), P(AXES), P(ab))
    return jax.shard_map(
        shards, mesh=finer, in_specs=in_specs, out_specs=P(AXES, None), check_vma=False
    )
```

time: 194 us -> 87 us (0.45)
  Pallas kernels: 0 us -> 83.4 us
  blocking collectives: 80.6 us -> 0 us
  waiting for transfers between devices: 57 us -> 0 us
  starting transfers between devices: 19.8 us -> 0 us
  matrix products: 17.9 us -> 0 us
  local copies, waits for them, and re-layouts: 16.7 us -> 3.42 us
    pallas_call x0 -> x1, Pallas kernels: none -> 83.4 us  [shards(): pl.pallas_call(kernel, out_shape=jax.ShapeDtypeStruct((4096, 128), f32),...]
    all_to_all x4 -> x0, blocking collectives: 80.6 us -> none  [the longest x1 58.3 us: shards(): lax.all_to_all(residual, AB, split_axis=0, concat_axis=1, tiled=True)]
    all_to_all x2 -> x0, waiting for transfers between devices: 57 us -> none  [copy_for_each(): lax.all_to_all(jnp.broadcast_to(array[None], (count, *array.shape)), axis...]
    all_to_all x2 -> x0, starting transfers between devices: 19.8 us -> none  [copy_for_each(): lax.all_to_all(jnp.broadcast_to(array[None], (count, *array.shape)), axis...]
    dot_general x1 -> x0, matrix products: 17.9 us -> none  [contract(): lax.dot_general(block_amps, integrals, (((1,), (1,)), ((), ())), precisio...]
    another operation x1 -> x0, local copies, waits for them, and re-layouts: 5.3 us -> none  [shards(): block_amps = grouped.reshape(-1, panel_cols)]
    broadcast_in_dim x4 -> x0, local copies, waits for them, and re-layouts: 4.22 us -> none  [copy_for_each(): jnp.broadcast_to(array[None], (count, *array.shape))]
    all_to_all x3 -> x0, local copies, waits for them, and re-layouts: 3.21 us -> none  [the longest x1 1.86 us: shards(): lax.all_to_all(residual, AB, split_axis=0, concat_axis=1, tiled=True)]
  transfers between devices with their start and end apart: 2 -> 0, of which waited for: 2 -> 0; matrix products, arithmetic and copies ran while one was open for 1% -> 0% of each run, Pallas kernels for 0% -> 0%
where the time goes in v1:
time: 87 us; the launch traced here: 86.8 us
  Pallas kernels  83.4 us (96%)
  local copies, waits for them, and re-layouts  3.42 us (4%)
    pallas_call x1, Pallas kernels, shards(): pl.pallas_call(kernel, out_shape=jax.ShapeDtypeStruct((4096, 128), f32),...  83.4 us
    unnamed x7, local copies, waits for them, and re-layouts  3.42 us

profile of v1, /device:TPU:1, one launch (start us, length us, event | category | flops | bytes accessed | tf_op | source)
XLA Modules:
  0.0 86.8 jit_solution(12292146603066457266)
XLA Ops:
  0.0 0.0 copy-start
  0.0 0.8 copy-done
  0.8 0.0 copy-start.1
  0.8 0.7 copy-done.1
  1.4 0.0 copy-start.2
  1.4 0.7 copy-done.2
  2.1 83.4 %shard_map.46 = f32[4096,128]{1,0:T(8,128)S(1)} custom-call(f32[8,1024]{1,0:T(8,128)S(1)} %copy-done, f32[1024,2048]{1,0:T(8,128)} %int_ref.1, f32[4]{0:T(128)S(1)} %copy-done.2, f32[8,128]{1,0:T(8,128)S(1)} %bitcast.7), custom_call_target="tpu_custom_call" | custom-call | tf_op jit(solution)/shard_map/pallas_call | solution.py:257
  85.5 1.3 %copy.7 = f32[4,131072]{1,0:T(4,128)} copy(f32[4,131072]{1,0:T(4,128)S(1)} %bitcast.6) | data formatting | bytes 4194304
Async XLA Ops:
  0.0 0.8 copy-start
  0.8 0.7 copy-start.1
  1.4 0.7 copy-start.2

commit v2 on v0

v2 whole, which is shorter than its diff:
```python
import jax
import jax.numpy as jnp
from jax import lax
from jax.experimental import pallas as pl
from jax.experimental.pallas import tpu as pltpu
from jax.sharding import Mesh
from jax.sharding import PartitionSpec as P

AXES = ("z", "y", "xh", "c", "xl")
MESH = pl.DeviceIdType.MESH

DIST = (1, 7, 2, 6, 3, 5, 4, 0)
PIECES = 8


def column(dy, dx):
    return dy % 4 + 4 * dx


def split(x):
    hi = x.astype(jnp.bfloat16)
    lo = (x - hi.astype(jnp.float32)).astype(jnp.bfloat16)
    return hi, lo


def kernel(
    amp_hbm, int_hbm, occ_hbm, vir_hbm, out_ref,
    amp, occ_ref, vir_ref, flat, etile, gath, ener, stage, bhi, blo, acat, res,
    in_sem, b_sem, z_send, z_recv, f_send, f_recv, c_send, c_recv,
    e_send, ez_recv, ef_recv, ec_recv, r_send, r_recv, own_sem,
):
    z, y, xh, c, xl = (lax.axis_index(a) for a in AXES)
    block = ((z * 4 + y) * 2 + xh) * 2 + c
    partner = (z, y, 1 - xh, c, 1 - xl)
    sibling = (z, y, xh, 1 - c, xl)

    def along_y(d):
        return (z, lax.rem(y + d, 4), xh, c, xl)

    inputs = [
        pltpu.make_async_copy(amp_hbm, amp, in_sem.at[0]),
        pltpu.make_async_copy(occ_hbm, occ_ref, in_sem.at[1]),
        pltpu.make_async_copy(vir_hbm, vir_ref, in_sem.at[2]),
    ]
    for copy in inputs:
        copy.start()

    def piece(i):
        rows = pl.ds(i * 128, 128)
        return pltpu.make_async_copy(int_hbm.at[rows, :], stage.at[rows, :], b_sem.at[i])

    for i in range(PIECES):
        piece(i).start()

    barrier = pltpu.get_barrier_semaphore()
    peers = [(lax.rem(z + d, 8), y, xh, c, xl) for d in range(1, 8)]
    peers += [(lax.rem(z + d, 8), y, xh, c, 1 - xl) for d in range(8)]
    peers += [along_y(d) for d in range(1, 4)]
    peers += [partner, sibling]
    for peer in peers:
        pl.semaphore_signal(barrier, inc=1, device_id=peer, device_id_type=MESH)

    for copy in inputs:
        copy.wait()
    for s in range(8):
        flat[pl.ds(s, 8, stride=8), :] = amp[:, pl.ds(s * 128, 128)]
    lane_row = lax.broadcasted_iota(jnp.int32, (8, 128), 0)
    energy = jnp.where(lane_row % 4 == 0, occ_ref[0], occ_ref[1])
    energy = jnp.where(lane_row % 4 == 2, occ_ref[2], energy)
    energy = jnp.where(lane_row % 4 == 3, occ_ref[3], energy)
    etile[...] = energy
    ener[0, 0, pl.ds(56, 8), :] = energy
    gath[0, 0, xl, pl.ds(224, 32), :] = flat[pl.ds(pl.multiple_of(xl * 32, 32), 32), :]

    def prepare(i):
        piece(i).wait()

        rows = pl.ds(i * 128, 128)
        hi, lo = split(stage[rows, :].T)
        bhi[:, rows] = hi
        blo[:, rows] = lo

    pl.semaphore_wait(barrier, len(peers))

    def remote(src, dst, send, recv, device):
        return pltpu.make_async_remote_copy(
            src_ref=src, dst_ref=dst, send_sem=send, recv_sem=recv,
            device_id=device, device_id_type=MESH,
        )

    def take(ref, recv):
        remote(ref, ref, own_sem, recv, sibling).wait_recv()

    for k, d in enumerate(DIST):
        zd = lax.rem(z + 8 - d, 8)
        rows = pl.ds(k * 32, 32)
        for j in (xl, 1 - xl) if d else (1 - xl,):
            remote(
                flat.at[pl.ds(pl.multiple_of(j * 32, 32), 32), :],
                gath.at[0, 0, xl, rows, :],
                z_send, z_recv.at[k // 4], (zd, y, xh, c, j),
            ).start()
        if d:
            remote(
                etile, ener.at[0, 0, pl.ds(k * 8, 8), :], e_send, ez_recv.at[k // 4],
                (zd, y, xh, c, xl),
            ).start()

    def part(col, core, run):
        return gath.at[col, core, :, pl.ds(run * 128, 128), :]

    def levels(col, core, run):
        return ener.at[col, core, pl.ds(run * 32, 32), :]

    def forward(col, run, to, device):
        remote(
            part(col, 0, run), part(to, 0, run), f_send, f_recv.at[to, run], device
        ).start()
        remote(
            levels(col, 0, run), levels(to, 0, run), e_send, ef_recv.at[to, run], device
        ).start()

    def arrived(col, run):
        take(part(col, 0, run), f_recv.at[col, run])
        take(levels(col, 0, run), ef_recv.at[col, run])

    def exchange(col, run):
        remote(part(col, 0, run), part(col, 1, run), c_send, c_recv.at[col, run], sibling).start()
        remote(
            levels(col, 0, run), levels(col, 1, run), e_send, ec_recv.at[col, run], sibling
        ).start()

    upper = lax.broadcasted_iota(jnp.int32, (2, 8, 128), 1) < 4
    home = pl.ds(pl.multiple_of(block * 32, 32), 32)

    def multiply(parts):
        m = 32 * len(parts)
        occ = []
        for i, (col, run) in enumerate(parts):
            take(part(col, 1, run), c_recv.at[col, run])
            take(levels(col, 1, run), ec_recv.at[col, run])
            for core in range(2):
                base = 32 * i + 16 * core
                for h in range(2):
                    for s in range(8):
                        rows = pl.ds(run * 128 + s, 16, stride=8)
                        hi, lo = split(gath[col, core, h, rows, :])
                        lanes = pl.ds((h * 8 + s) * 128, 128)
                        acat[pl.ds(base, 16), lanes] = hi
                        acat[pl.ds(m + base, 16), lanes] = lo
                pairs = ener[col, core, pl.ds(run * 32, 32), :].reshape(2, 2, 8, 128)
                occ.append(jnp.where(upper, pairs[:, 0], pairs[:, 1]))

        for nb in range(4):
            lanes = pl.ds(nb * 256, 256)
            high = jnp.dot(
                acat[pl.ds(0, 2 * m), :], bhi[:, lanes], preferred_element_type=jnp.float32
            )
            low = jnp.dot(
                acat[pl.ds(0, m), :], blo[:, lanes], preferred_element_type=jnp.float32
            )
            total = high[:m] + (high[m:] + low)
            for i, (col, run) in enumerate(parts):
                for core in range(2):
                    base = 32 * i + 16 * core
                    tiles = []
                    for t in range(2):
                        value = total[base : base + 16, 128 * t : 128 * t + 128]
                        vir = vir_ref[pl.ds(nb * 2 + t, 1), :]
                        tiles.append(
                            value.reshape(2, 8, 128) / (vir[None] - occ[2 * i + core])
                        )
                    even = jnp.where(upper, tiles[0], pltpu.roll(tiles[1], 4, 1))
                    odd = jnp.where(upper, pltpu.roll(tiles[0], 4, 1), tiles[1])
                    for b in range(2):
                        k = 4 * run + 2 * b
                        res[col, core, k, pl.ds(nb * 8, 8), :] = even[b]
                        res[col, core, k + 1, pl.ds(nb * 8, 8), :] = odd[b]

    def give(col, slots):
        yd = lax.rem(y + col % 4, 4)
        xhd, xld = (1 - xh, 1 - xl) if col >= 4 else (xh, xl)
        for k in slots:
            zd = lax.rem(z + DIST[k], 8)
            for core in range(2):
                if col == 0 and core == 0 and DIST[k] == 0:
                    continue
                cd = 1 - c if core else c
                remote(
                    res.at[col, core, k], out_ref.at[home, :], r_send, r_recv,
                    (zd, yd, xhd, cd, xld),
                ).start()

    here, up, far, down = (column(d, 0) for d in range(4))
    over, up_over, far_over, down_over = (column(d, 1) for d in range(4))
    near_slots, far_slots = (2, 3, 0, 1), (6, 4, 5, 7)
    all_slots = (6, 4, 5, 2, 3, 0, 1, 7)

    prepare(0)
    prepare(1)
    prepare(2)
    for run in range(2):
        take(gath.at[0, 0, :, pl.ds(0, 112 if run else 128), :], z_recv.at[run])
        take(ener.at[0, 0, pl.ds(0, 24 if run else 32), :], ez_recv.at[run])
        exchange(here, run)
        forward(here, run, over, partner)
        forward(here, run, down, along_y(1))
        forward(here, run, up, along_y(3))
        if run == 0:
            for i in range(3, 8):
                prepare(i)
        multiply([(here, run)])
        give(here, (6, 4, 5, 7) if run else (2, 3, 0, 1))
    for run in range(2):
        arrived(over, run)
        exchange(over, run)
        for col in (up, down):
            arrived(col, run)
            exchange(col, run)
        if run == 0:
            forward(down, 0, far, along_y(1))
        else:
            forward(up, 1, far, along_y(3))
        forward(over, run, down_over, along_y(1))
        forward(over, run, up_over, along_y(3))
        multiply([(over, run)])
        give(over, (6, 4, 5, 7) if run else (2, 3, 0, 1))
    for run in range(2):
        arrived(far, run)
        exchange(far, run)
        forward(far, run, far_over, partner)
    multiply([(far, 0), (far, 1)])
    give(far, all_slots)
    for run in range(2):
        for col in (up_over, down_over):
            arrived(col, run)
            exchange(col, run)
    multiply([(up_over, 0), (up_over, 1), (down_over, 0), (down_over, 1)])
    give(up_over, all_slots)
    give(down_over, all_slots)
    for run in range(2):
        arrived(far_over, run)
        exchange(far_over, run)
    multiply([(far_over, 0), (far_over, 1)])
    give(far_over, all_slots)
    multiply([(up, 0), (up, 1), (down, 0), (down, 1)])
    give(up, all_slots)
    give(down, all_slots)

    own = pltpu.make_async_copy(res.at[0, 0, 7], out_ref.at[home, :], own_sem)
    own.start()
    own.wait()

    def sent(ref, send):
        remote(ref, ref, send, own_sem, sibling).wait_send()

    sent(gath.at[0, 0, :, pl.ds(0, 240), :], z_send)
    sent(gath.at[pl.ds(0, 7), 0], f_send)
    sent(gath.at[:, 0], c_send)
    sent(ener.at[0, 0, pl.ds(0, 56), :], e_send)
    sent(ener.at[pl.ds(0, 7), 0], e_send)
    sent(ener.at[:, 0], e_send)
    sent(out_ref.at[pl.ds(0, 127 * 32), :], r_send)
    take(out_ref.at[pl.ds(0, 127 * 32), :], r_recv)


def shards(amplitudes, integrals, occ_pairs, vir_pairs):
    f32, bf16 = jnp.float32, jnp.bfloat16
    dma = pltpu.SemaphoreType.DMA
    out = pl.pallas_call(
        kernel,
        out_shape=jax.ShapeDtypeStruct((4096, 128), f32),
        in_specs=[pl.BlockSpec(memory_space=pltpu.HBM)] * 4,
        out_specs=pl.BlockSpec(memory_space=pl.ANY),
        scratch_shapes=[
            pltpu.VMEM((8, 1024), f32),
            pltpu.SMEM((4,), f32),
            pltpu.VMEM((8, 128), f32),
            pltpu.VMEM((64, 128), f32),
            pltpu.VMEM((8, 128), f32),
            pltpu.VMEM((8, 2, 2, 256, 128), f32),
            pltpu.VMEM((8, 2, 64, 128), f32),
            pltpu.VMEM((1024, 2048), f32),
            pltpu.VMEM((2048, 1024), bf16),
            pltpu.VMEM((2048, 1024), bf16),
            pltpu.VMEM((256, 2048), bf16),
            pltpu.VMEM((8, 2, 8, 32, 128), f32),
            dma((3,)), dma((PIECES,)),
            dma, dma((2,)), dma, dma((8, 2)), dma, dma((8, 2)),
            dma, dma((2,)), dma((8, 2)), dma((8, 2)), dma, dma, dma,
        ],
        compiler_params=pltpu.CompilerParams(
            collective_id=0, has_side_effects=True, vmem_limit_bytes=56 << 20
        ),
    )(amplitudes, integrals, occ_pairs, vir_pairs.reshape(8, 128))
    return out.reshape(1024, 4, 128).transpose(1, 0, 2).reshape(4, 131072)


def solution(mesh):
    finer = Mesh(mesh.devices.reshape(8, 4, 2, 2, 2), AXES)
    ab = ("z", "y", "xh", "c")
    in_specs = (P(ab, "xl"), P(ab, None), P(AXES), P(ab))
    return jax.shard_map(
        shards, mesh=finer, in_specs=in_specs, out_specs=P(AXES, None), check_vma=False
    )
```

time: 194 us -> 74.9 us (0.39)
  blocking collectives: 80.6 us -> 0 us
  Pallas kernels: 0 us -> 71.7 us
  waiting for transfers between devices: 57 us -> 0 us
  starting transfers between devices: 19.8 us -> 0 us
  matrix products: 17.9 us -> 0 us
  local copies, waits for them, and re-layouts: 16.7 us -> 3.05 us
    all_to_all x4 -> x0, blocking collectives: 80.6 us -> none  [the longest x1 58.3 us: shards(): lax.all_to_all(residual, AB, split_axis=0, concat_axis=1, tiled=True)]
    pallas_call x0 -> x1, Pallas kernels: none -> 71.7 us  [shards(): pl.pallas_call(kernel, out_shape=jax.ShapeDtypeStruct((4096, 128), f32),...]
    all_to_all x2 -> x0, waiting for transfers between devices: 57 us -> none  [copy_for_each(): lax.all_to_all(jnp.broadcast_to(array[None], (count, *array.shape)), axis...]
    all_to_all x2 -> x0, starting transfers between devices: 19.8 us -> none  [copy_for_each(): lax.all_to_all(jnp.broadcast_to(array[None], (count, *array.shape)), axis...]
    dot_general x1 -> x0, matrix products: 17.9 us -> none  [contract(): lax.dot_general(block_amps, integrals, (((1,), (1,)), ((), ())), precisio...]
    another operation x1 -> x0, local copies, waits for them, and re-layouts: 5.3 us -> none  [shards(): block_amps = grouped.reshape(-1, panel_cols)]
    broadcast_in_dim x4 -> x0, local copies, waits for them, and re-layouts: 4.22 us -> none  [copy_for_each(): jnp.broadcast_to(array[None], (count, *array.shape))]
    all_to_all x3 -> x0, local copies, waits for them, and re-layouts: 3.21 us -> none  [the longest x1 1.86 us: shards(): lax.all_to_all(residual, AB, split_axis=0, concat_axis=1, tiled=True)]
  transfers between devices with their start and end apart: 2 -> 0, of which waited for: 2 -> 0; matrix products, arithmetic and copies ran while one was open for 1% -> 0% of each run, Pallas kernels for 0% -> 0%
where the time goes in v2:
time: 74.9 us; the launch traced here: 74.8 us
  Pallas kernels  71.7 us (96%)
  local copies, waits for them, and re-layouts  3.05 us (4%)
    pallas_call x1, Pallas kernels, shards(): pl.pallas_call(kernel, out_shape=jax.ShapeDtypeStruct((4096, 128), f32),...  71.7 us
    unnamed x1, local copies, waits for them, and re-layouts  3.05 us

profile of v2, /device:TPU:1, one launch (start us, length us, event | category | flops | bytes accessed | tf_op | source)
XLA Modules:
  0.0 74.8 jit_solution(3371204317665884226)
XLA Ops:
  0.0 71.7 %shard_map.46 = f32[4096,128]{1,0:T(8,128)} custom-call(f32[8,1024]{1,0:T(8,128)} %amp_hbm.1, f32[1024,2048]{1,0:T(8,128)} %int_hbm.1, f32[4]{0:T(128)} %occ_hbm.1, f32[8,128]{1,0:T(8,128)} %bitcast.7), custom_call_target="tpu_custom_call" | custom-call | tf_op jit(solution)/shard_map/pallas_call | solution.py:270
  71.7 3.0 %copy.7 = f32[4,131072]{1,0:T(4,128)} copy(f32[4,131072]{1,0:T(4,128)} %bitcast.6) | data formatting | bytes 4194304

commit v3 on v2

--- a/solution.py
+++ b/solution.py
@@ -196,9 +196,8 @@
     near_slots, far_slots = (2, 3, 0, 1), (6, 4, 5, 7)
     all_slots = (6, 4, 5, 2, 3, 0, 1, 7)
 
-    prepare(0)
-    prepare(1)
-    prepare(2)
+    for i in range(6):
+        prepare(i)
     for run in range(2):
         take(gath.at[0, 0, :, pl.ds(0, 112 if run else 128), :], z_recv.at[run])
         take(ener.at[0, 0, pl.ds(0, 24 if run else 32), :], ez_recv.at[run])
@@ -207,7 +206,7 @@
         forward(here, run, down, along_y(1))
         forward(here, run, up, along_y(3))
         if run == 0:
-            for i in range(3, 8):
+            for i in range(6, 8):
                 prepare(i)
         multiply([(here, run)])
         give(here, (6, 4, 5, 7) if run else (2, 3, 0, 1))
@@ -269,7 +268,7 @@
     dma = pltpu.SemaphoreType.DMA
     out = pl.pallas_call(
         kernel,
-        out_shape=jax.ShapeDtypeStruct((4096, 128), f32),
+        out_shape=pltpu.VMEM((4096, 128), f32),
         in_specs=[pl.BlockSpec(memory_space=pltpu.HBM)] * 4,
         out_specs=pl.BlockSpec(memory_space=pl.ANY),
         scratch_shapes=[

time: 74.9 us -> 73.1 us (0.976)
  local copies, waits for them, and re-layouts: 3.05 us -> 1.32 us
    unnamed x1, local copies, waits for them, and re-layouts: 3.05 us -> 1.32 us
where the time goes in v3:
time: 73.1 us; the launch traced here: 73 us
  Pallas kernels  71.7 us (98%)
  local copies, waits for them, and re-layouts  1.32 us (2%)
    pallas_call x1, Pallas kernels, shards(): pl.pallas_call(kernel, out_shape=pltpu.VMEM((4096, 128), f32), in_specs=[...  71.7 us

profile of v3, /device:TPU:1, one launch (start us, length us, event | category | flops | bytes accessed | tf_op | source)
XLA Modules:
  0.0 73.0 jit_solution(15218003264402670809)
XLA Ops:
  0.0 71.7 %shard_map.46 = f32[4096,128]{1,0:T(8,128)S(1)} custom-call(f32[8,1024]{1,0:T(8,128)} %amp_hbm.1, f32[1024,2048]{1,0:T(8,128)} %int_hbm.1, f32[4]{0:T(128)} %occ_hbm.1, f32[8,128]{1,0:T(8,128)} %bitcast.7), custom_call_target="tpu_custom_call" | custom-call | tf_op jit(solution)/shard_map/pallas_call | solution.py:269
  71.7 1.3 %copy.7 = f32[4,131072]{1,0:T(4,128)} copy(f32[4,131072]{1,0:T(4,128)S(1)} %bitcast.6) | data formatting | bytes 4194304

commit v4 on v3

--- a/solution.py
+++ b/solution.py
@@ -228,15 +228,15 @@
         arrived(far, run)
         exchange(far, run)
         forward(far, run, far_over, partner)
-    multiply([(far, 0), (far, 1)])
-    give(far, all_slots)
-    for run in range(2):
-        for col in (up_over, down_over):
+        multiply([(far, run)])
+        give(far, (6, 4, 5, 7) if run else (2, 3, 0, 1))
+    for col in (up_over, down_over):
+        for run in range(2):
             arrived(col, run)
             exchange(col, run)
-    multiply([(up_over, 0), (up_over, 1), (down_over, 0), (down_over, 1)])
-    give(up_over, all_slots)
-    give(down_over, all_slots)
+    for col in (up_over, down_over):
+        multiply([(col, 0), (col, 1)])
+        give(col, all_slots)
     for run in range(2):
         arrived(far_over, run)
         exchange(far_over, run)

time: 73.1 us -> 72.1 us (0.986)
  Pallas kernels: 71.7 us -> 70.7 us
    pallas_call x1, Pallas kernels: 71.7 us -> 70.7 us  [shards(): pl.pallas_call(kernel, out_shape=pltpu.VMEM((4096, 128), f32), in_specs=[...]
where the time goes in v4:
time: 72.1 us; the launch traced here: 72 us
  Pallas kernels  70.7 us (98%)
  local copies, waits for them, and re-layouts  1.32 us (2%)
    pallas_call x1, Pallas kernels, shards(): pl.pallas_call(kernel, out_shape=pltpu.VMEM((4096, 128), f32), in_specs=[...  70.7 us

profile of v4, /device:TPU:1, one launch (start us, length us, event | category | flops | bytes accessed | tf_op | source)
XLA Modules:
  0.0 72.0 jit_solution(5012174931977958680)
XLA Ops:
  0.0 70.7 %shard_map.46 = f32[4096,128]{1,0:T(8,128)S(1)} custom-call(f32[8,1024]{1,0:T(8,128)} %amp_hbm.1, f32[1024,2048]{1,0:T(8,128)} %int_hbm.1, f32[4]{0:T(128)} %occ_hbm.1, f32[8,128]{1,0:T(8,128)} %bitcast.7), custom_call_target="tpu_custom_call" | custom-call | tf_op jit(solution)/shard_map/pallas_call | solution.py:269
  70.7 1.3 %copy.7 = f32[4,131072]{1,0:T(4,128)} copy(f32[4,131072]{1,0:T(4,128)S(1)} %bitcast.6) | data formatting | bytes 4194304

commit v5 on v4

--- a/solution.py
+++ b/solution.py
@@ -133,7 +133,7 @@
     upper = lax.broadcasted_iota(jnp.int32, (2, 8, 128), 1) < 4
     home = pl.ds(pl.multiple_of(block * 32, 32), 32)
 
-    def multiply(parts):
+    def multiply(parts, early=()):
         m = 32 * len(parts)
         occ = []
         for i, (col, run) in enumerate(parts):
@@ -176,8 +176,13 @@
                         k = 4 * run + 2 * b
                         res[col, core, k, pl.ds(nb * 8, 8), :] = even[b]
                         res[col, core, k + 1, pl.ds(nb * 8, 8), :] = odd[b]
-
-    def give(col, slots):
+            if early and nb % 2:
+                give(parts[0][0], early, nb // 2)
+
+    def give(col, slots, half=None):
+        cut = pl.ds(0, 32) if half is None else pl.ds(half * 16, 16)
+        start = block * 32 if half is None else block * 32 + half * 16
+        place = pl.ds(pl.multiple_of(start, 16), 32 if half is None else 16)
         yd = lax.rem(y + col % 4, 4)
         xhd, xld = (1 - xh, 1 - xl) if col >= 4 else (xh, xl)
         for k in slots:
@@ -187,7 +192,7 @@
                     continue
                 cd = 1 - c if core else c
                 remote(
-                    res.at[col, core, k], out_ref.at[home, :], r_send, r_recv,
+                    res.at[col, core, k, cut, :], out_ref.at[place, :], r_send, r_recv,
                     (zd, yd, xhd, cd, xld),
                 ).start()
 
@@ -208,8 +213,7 @@
         if run == 0:
             for i in range(6, 8):
                 prepare(i)
-        multiply([(here, run)])
-        give(here, (6, 4, 5, 7) if run else (2, 3, 0, 1))
+        multiply([(here, run)], (6, 4, 5, 7) if run else (2, 3, 0, 1))
     for run in range(2):
         arrived(over, run)
         exchange(over, run)

time: 72.1 us -> 72.1 us (level)
  no operation moved by 1% of the time
where the time goes in v5:
time: 72.1 us; the launch traced here: 72 us
  Pallas kernels  70.7 us (98%)
  local copies, waits for them, and re-layouts  1.32 us (2%)
    pallas_call x1, Pallas kernels, shards(): pl.pallas_call(kernel, out_shape=pltpu.VMEM((4096, 128), f32), in_specs=[...  70.7 us

profile of v5, /device:TPU:1, one launch (start us, length us, event | category | flops | bytes accessed | tf_op | source)
XLA Modules:
  0.0 72.0 jit_solution(9069735313217130422)
XLA Ops:
  0.0 70.7 %shard_map.46 = f32[4096,128]{1,0:T(8,128)S(1)} custom-call(f32[8,1024]{1,0:T(8,128)} %amp_hbm.1, f32[1024,2048]{1,0:T(8,128)} %int_hbm.1, f32[4]{0:T(128)} %occ_hbm.1, f32[8,128]{1,0:T(8,128)} %bitcast.7), custom_call_target="tpu_custom_call" | custom-call | tf_op jit(solution)/shard_map/pallas_call | solution.py:273
  70.7 1.3 %copy.7 = f32[4,131072]{1,0:T(4,128)} copy(f32[4,131072]{1,0:T(4,128)S(1)} %bitcast.6) | data formatting | bytes 4194304
